TPU v7x, 256 devices: a whole 4x4x8 slice. The times are simulated.
256 devices in a mesh: segment: 8 (over z), tile: 32 (over x, y, core).
Axes of the slice: x: 4, y: 4, z: 8, core: 2. Of those that a mesh axis runs over, the one named last changes fastest.
Arguments:
- latent: bfloat16 [4, 8, 128, 384], P(None, None, 'tile'), may hold values from -6 to 6
- frame_order: int32 [4], replicated, may hold values from 0 to 3, each once
- section_weight: bfloat16 [8, 27, 384, 384], P('segment'), may hold values from -0.0625 to 0.0625
- section_gain: bfloat16 [8, 384], P('segment'), may hold values from 0.5 to 1.5
- up_weight: bfloat16 [27, 384, 192], P(None, 'tile'), may hold values from -0.0625 to 0.0625
- reward_weight: bfloat16 [49152, 1280], P(None, 'tile'), may hold values from -0.02734375 to 0.02734375
- reward_coef: float32 [1280], P('tile'), may hold values from -6 to 6
Outputs:
- input_grads: float32 [8, 4, 8, 128, 384], P('segment', None, None, 'tile')
All inputs are finite; a program needn't handle non-finite values.
Results may differ from a plain program's by a relative error of at most 0.03.
Values may be sent and summed in bfloat16 or wider, within the bound.
No kernel may reach another device: no remote copies, remote signals or barrier semaphores. Data moves between devices by JAX's collectives and lax.ppermute only.
A program may use at most 128 MiB of HBM per device.

v0:
```python
import jax
import jax.numpy as jnp
from jax import lax
from jax.sharding import PartitionSpec as P

P_SIZE = 16
EPS = 1e-06


def with_halo(cells, sides, width):
    for axis, dim in sides:
        count = lax.axis_size(axis)
        ends = count - 1
        head = lax.slice_in_dim(cells, 0, width, axis=dim)
        tail = lax.slice_in_dim(cells, cells.shape[dim] - width, cells.shape[dim], axis=dim)
        cells = jnp.concatenate(
            [
                lax.ppermute(tail, axis, [(i, (i + 1) % count) for i in range(ends)]),
                cells,
                lax.ppermute(head, axis, [((i + 1) % count, i) for i in range(ends)]),
            ],
            axis=dim,
        )
    return cells


def from_behind(block, axis, distance):
    devices = range(lax.axis_size(axis))
    route = [(i - distance, i) for i in devices if i - distance in devices]
    return lax.ppermute(block, axis, route)


def section_act(inputs, gain_row):
    as_float = inputs.astype(jnp.float32)
    inv_norm = lax.rsqrt(jnp.mean(as_float * as_float, axis=-1, keepdims=True) + EPS)
    return jax.nn.silu(as_float * inv_norm * gain_row.astype(jnp.float32))


def causal_taps(stacked, height, width):
    pieces = []
    for time_off in range(3):
        for row_off in range(3):
            for col_off in range(3):
                pieces.append(
                    stacked[time_off, row_off : row_off + height, col_off : col_off + width]
                )
    return jnp.stack(pieces, axis=2).reshape(height * width, -1)


def reverse_taps(stacked, height, width):
    pieces = []
    for time_off in range(3):
        for row_off in range(3):
            for col_off in range(3):
                pieces.append(
                    stacked[
                        time_off,
                        2 - row_off : 2 - row_off + height,
                        2 - col_off : 2 - col_off + width,
                    ]
                )
    return jnp.stack(pieces, axis=2).reshape(height * width, -1)


def plane_taps(plane, height, width):
    pieces = []
    for row_off in range(3):
        for col_off in range(3):
            pieces.append(
                plane[2 - row_off : 2 - row_off + height, 2 - col_off : 2 - col_off + width]
            )
    return jnp.stack(pieces, axis=2).reshape(height * width, -1)


def pad_rows(stacked):
    return jnp.pad(stacked, ((0, 0), (1, 1), (0, 0), (0, 0)))


def on_device(
    latent, frame_order, section_weight, section_gain, up_weight, reward_weight, reward_coef
):
    segment_count = lax.axis_size("segment")
    segment_at = lax.axis_index("segment")
    frame_count, height, width_dev, channels = latent.shape
    weight_fwd = section_weight[0].reshape(27 * channels, channels)
    weight_back = section_weight[0].transpose(0, 2, 1).reshape(27 * channels, channels)
    gain_row = section_gain[0]
    is_first = segment_at == 0
    is_last = segment_at == segment_count - 1
    tick_count = frame_count + segment_count - 1
    zero_rim = jnp.zeros((height, width_dev + 2, channels), jnp.bfloat16)
    zero_frames = jnp.zeros((frame_count, height, width_dev, channels), jnp.bfloat16)

    def forward_tick(loop_step, carried):
        prev_two, prev_one, incoming, inputs_kept, outputs_kept = carried
        frame_slot = loop_step - segment_at
        is_live = (frame_slot >= 0) & (frame_slot < frame_count)
        frame_at = jnp.clip(frame_slot, 0, frame_count - 1)
        own_frame = lax.dynamic_index_in_dim(latent, frame_order[frame_at], 0, keepdims=False)
        segment_in = jnp.where(is_first, own_frame, incoming)
        activated = section_act(segment_in, gain_row).astype(jnp.bfloat16)
        act_rim = with_halo(activated, (("tile", 1),), 1)
        window = pad_rows(jnp.stack([prev_two, prev_one, act_rim]))

        def live_conv():
            return jnp.dot(
                causal_taps(window, height, width_dev),
                weight_fwd,
                preferred_element_type=jnp.float32,
            )

        def dead_conv():
            return jnp.zeros((height * width_dev, channels), jnp.float32)

        conv_out = lax.cond(is_live, live_conv, dead_conv)
        segment_out = (
            segment_in.astype(jnp.float32) + conv_out.reshape(height, width_dev, channels)
        ).astype(jnp.bfloat16)
        prev_two = jnp.where(is_live, prev_one, prev_two)
        prev_one = jnp.where(is_live, act_rim, prev_one)
        inputs_kept = jnp.where(is_live, inputs_kept.at[frame_at].set(segment_in), inputs_kept)
        outputs_kept = jnp.where(is_live, outputs_kept.at[frame_at].set(segment_out), outputs_kept)
        incoming = from_behind(segment_out, "segment", 1)
        return (prev_two, prev_one, incoming, inputs_kept, outputs_kept)

    start_fwd = (
        zero_rim,
        zero_rim,
        jnp.zeros((height, width_dev, channels), jnp.bfloat16),
        zero_frames,
        zero_frames,
    )
    carried = lax.fori_loop(0, tick_count, forward_tick, start_fwd)
    inputs_kept = carried[3]
    outputs_kept = carried[4]
    gathered_up = lax.all_gather(up_weight, "tile", axis=1, tiled=True)
    up_width = gathered_up.shape[2]
    up_flat = gathered_up.reshape(27 * channels, up_width)
    back_up = (
        gathered_up.reshape(3, 9, channels, up_width)
        .transpose(1, 3, 0, 2)
        .reshape(9 * up_width, 3 * channels)
    )
    padded_deep = jnp.concatenate(
        [jnp.zeros((2, height, width_dev, channels), jnp.bfloat16), outputs_kept], 0
    )
    collected = jnp.zeros((frame_count + 2, height, width_dev, channels), jnp.float32)
    for frame_slot in range(frame_count):
        head_window = lax.dynamic_slice_in_dim(padded_deep, frame_slot, 3, 0)
        widened = with_halo(
            jnp.repeat(jnp.repeat(head_window, 2, axis=1), 2, axis=2), (("tile", 2),), 1
        )
        preact = jnp.dot(
            causal_taps(pad_rows(widened), 2 * height, 2 * width_dev),
            up_flat,
            preferred_element_type=jnp.float32,
        )
        preact = preact.reshape(2 * height, 2 * width_dev, up_width)
        features = jax.nn.silu(preact).astype(jnp.bfloat16)
        gathered = lax.all_gather(
            features.reshape(2 * height, 2 * width_dev * up_width), "tile", axis=1, tiled=True
        )
        full_width = gathered.shape[1] // up_width
        patches = (
            gathered.reshape(2 * height // P_SIZE, P_SIZE, full_width // P_SIZE, P_SIZE, up_width)
            .transpose(0, 2, 1, 3, 4)
            .reshape(-1, P_SIZE * P_SIZE * up_width)
        )
        logits = jnp.dot(patches, reward_weight, preferred_element_type=jnp.float32)
        squashed = jnp.tanh(logits)
        logit_grad = (reward_coef * (1.0 - squashed * squashed)).astype(jnp.bfloat16)
        patch_grad = lax.dot_general(
            logit_grad, reward_weight, (((1,), (1,)), ((), ())), preferred_element_type=jnp.float32
        )
        patch_back = patch_grad.reshape(
            2 * height // P_SIZE, full_width // P_SIZE, P_SIZE, P_SIZE, up_width
        ).transpose(0, 2, 1, 3, 4)
        patch_back = patch_back.reshape(2 * height, full_width * up_width)
        feat_grad = (
            lax.psum_scatter(
                patch_back.astype(jnp.bfloat16), "tile", scatter_dimension=1, tiled=True
            )
            .astype(jnp.float32)
            .reshape(2 * height, 2 * width_dev, up_width)
        )
        sigmoid_p = jax.nn.sigmoid(preact)
        preact_grad = (feat_grad * sigmoid_p * (1.0 + preact * (1.0 - sigmoid_p))).astype(
            jnp.bfloat16
        )
        grad_rim_up = with_halo(preact_grad, (("tile", 1),), 1)
        grad_pad = jnp.pad(grad_rim_up, ((1, 1), (0, 0), (0, 0)))
        contribution = jnp.dot(
            plane_taps(grad_pad, 2 * height, 2 * width_dev),
            back_up,
            preferred_element_type=jnp.float32,
        )
        contribution = contribution.reshape(height, 2, width_dev, 2, 3, channels).sum(axis=(1, 3))
        frame_map = (
            jnp.arange(frame_count + 2)[None, :] == (frame_slot + jnp.arange(3))[:, None]
        ).astype(jnp.float32)
        produced = jnp.einsum("dk,hwdc->khwc", frame_map, contribution)
        collected = collected + jnp.where(is_last, produced, 0.0)
    deep_grad = collected[2:]

    def backward_tick(loop_step, carried):
        next_one, next_two, incoming, grads_kept = carried
        frame_slot = loop_step - (segment_count - 1 - segment_at)
        is_live = (frame_slot >= 0) & (frame_slot < frame_count)
        frame_at = frame_count - 1 - jnp.clip(frame_slot, 0, frame_count - 1)
        own_grad = lax.dynamic_index_in_dim(deep_grad, frame_at, 0, keepdims=False)
        grad_out = jnp.where(is_last, own_grad, incoming)
        grad_rim = with_halo(grad_out.astype(jnp.bfloat16), (("tile", 1),), 1)
        window = pad_rows(jnp.stack([next_two, next_one, grad_rim]))
        segment_in = lax.dynamic_index_in_dim(inputs_kept, frame_at, 0, keepdims=False)

        def live_back():
            conv_back = jnp.dot(
                reverse_taps(window, height, width_dev),
                weight_back,
                preferred_element_type=jnp.float32,
            )
            _, pullback = jax.vjp(
                lambda values: section_act(values, gain_row), segment_in.astype(jnp.float32)
            )
            return pullback(conv_back.reshape(height, width_dev, channels))[0]

        def dead_back():
            return jnp.zeros((height, width_dev, channels), jnp.float32)

        grad_in = grad_out + lax.cond(is_live, live_back, dead_back)
        next_two = jnp.where(is_live, next_one, next_two)
        next_one = jnp.where(is_live, grad_rim, next_one)
        grads_kept = jnp.where(is_live, grads_kept.at[frame_at].set(grad_in), grads_kept)
        incoming = from_behind(grad_in.astype(jnp.bfloat16), "segment", -1).astype(grad_in.dtype)
        return (next_one, next_two, incoming, grads_kept)

    start_bwd = (
        zero_rim,
        zero_rim,
        jnp.zeros((height, width_dev, channels), jnp.float32),
        jnp.zeros((frame_count, height, width_dev, channels), jnp.float32),
    )
    carried = lax.fori_loop(0, tick_count, backward_tick, start_bwd)
    return carried[3][None]


def solution(mesh):
    in_specs = (
        P(None, None, "tile", None),
        P(),
        P("segment", None, None, None),
        P("segment", None),
        P(None, "tile", None),
        P(None, "tile"),
        P("tile"),
    )
    out_specs = P("segment", None, None, "tile", None)
    return jax.shard_map(
        on_device, mesh=mesh, in_specs=in_specs, out_specs=out_specs, check_vma=False
    )
```

profile of v0, /device:TPU:2, one launch (start us, length us, event | category | flops | bytes accessed | tf_op | source)
XLA Modules:
  0.0 1193.0 jit_solution(10508438219004715807)
XLA Ops:
  7.3 270.5 %while.49 = (s32[]{:T(128)}, bf16[8,6,384]{2,0,1:T(8,128)(2,1)S(1)}, bf16[8,6,384]{2,0,1:T(8,128)(2,1)S(1)}, bf16[8,4,384]{2,0,1:T(8,128)(2,1)S(1)}, bf16[4,8,4,...) while((s32[]{:T(128)}, ...), condition=%wide.region_5.6_spmd.clone, body=%wide.region_0.5_spmd.clone.sunk | while | flops 255259072 | bytes 13963990 | solution.py:133
  127.0 9.3 collective-permute-start.2
  219.4 7.1 collective-permute-start.2
  265.8 10.5 collective-permute-start.2
  336.4 25.2 %all-gather.6.cloned.1.call-done = bf16[27,384,192]{2,0,1:T(8,128)(2,1)} async-done(((bf16[27,12,192]{2,0,1:T(8,128)(2,1)}), bf16[27,384,192]{2,0,1:T(8,128)(2,1)}) %all-gather.6.cloned.1.call-update) | async-done | bytes 3981328 | tf_op jit(solution)/shard_map/all_gather | solution.py:136
  361.6 10.1 multiply_convert_fusion.7
  382.8 10.1 multiply_convert_fusion.5
  404.0 9.5 multiply_convert_fusion.3
  423.9 9.4 multiply_convert_fusion.1
  443.2 7.4 convolution_convert_fusion.3
  460.7 9.4 all-gather.10.cloned.1.call-done
  478.9 7.3 convolution_convert_fusion.2
  496.2 23.6 %all-gather.12.cloned.1.call-done = bf16[16,49152]{1,0:T(8,128)(2,1)} async-done(((bf16[16,1536]{1,0:T(8,128)(2,1)}), bf16[16,49152]{1,0:T(8,128)(2,1)}) %all-gather.12.cloned.1.call-update) | async-done | bytes 1572880 | tf_op jit(solution)/shard_map/all_gather | solution.py:160
  528.7 7.3 convolution_convert_fusion.1
  546.2 23.4 %all-gather.14.cloned.1.call-done = bf16[16,49152]{1,0:T(8,128)(2,1)} async-done(((bf16[16,1536]{1,0:T(8,128)(2,1)}), bf16[16,49152]{1,0:T(8,128)(2,1)}) %all-gather.14.cloned.1.call-update) | async-done | bytes 1572880 | tf_op jit(solution)/shard_map/all_gather | solution.py:160
  578.5 7.3 convolution_convert_fusion
  595.6 11.7 copy.635
  607.3 8.6 copy.533
  630.7 28.2 %reduce-scatter.5.cloned.1.call-done = bf16[16,1536]{1,0:T(8,128)(2,1)} async-done(((bf16[16,49152]{1,0:T(8,128)(2,1)}), bf16[16,1536]{1,0:T(8,128)(2,1)}) %reduce-scatter.5.cloned.1.call-update) | async-done | bytes 49168 | tf_op jit(solution)/shard_map/reduce_scatter | solution.py:180
  667.6 80.6 %reduce-scatter.7.cloned.1.call-done = bf16[16,1536]{1,0:T(8,128)(2,1)} async-done(((bf16[16,49152]{1,0:T(8,128)(2,1)}), bf16[16,1536]{1,0:T(8,128)(2,1)}) %reduce-scatter.7.cloned.1.call-update) | async-done | bytes 49168 | tf_op jit(solution)/shard_map/reduce_scatter | solution.py:180
  756.9 80.6 %reduce-scatter.9.cloned.1.call-done = bf16[16,1536]{1,0:T(8,128)(2,1)} async-done(((bf16[16,49152]{1,0:T(8,128)(2,1)}), bf16[16,1536]{1,0:T(8,128)(2,1)}) %reduce-scatter.9.cloned.1.call-update) | async-done | bytes 49168 | tf_op jit(solution)/shard_map/reduce_scatter | solution.py:180
  838.6 88.3 %reduce-scatter.11.cloned.1.call-done = bf16[16,1536]{1,0:T(8,128)(2,1)} async-done(((bf16[16,49152]{1,0:T(8,128)(2,1)}), bf16[16,1536]{1,0:T(8,128)(2,1)}) %reduce-scatter.11.cloned.1.call-update) | async-done | bytes 49168 | tf_op jit(solution)/shard_map/reduce_scatter | solution.py:180
  964.4 221.2 %while.50 = (s32[]{:T(128)}, bf16[8,6,384]{2,0,1:T(8,128)(2,1)S(1)}, bf16[8,6,384]{2,0,1:T(8,128)(2,1)S(1)}, f32[8,4,384]{2,0,1:T(8,128)S(1)}, f32[4,8,4,384]{3,...) while((s32[]{:T(128)}, ...), condition=%wide.region_20.21_spmd.clone, body=%wide.region_14.20_spmd.clone.sunk | while | flops 255418992 | bytes 14603769 | solution.py:243
  1067.3 33.6 %collective-permute-done.5 = bf16[8,4,384]{2,0,1:T(8,128)(2,1)S(1)} collective-permute-done((bf16[8,4,384]{2,0,1:T(8,128)(2,1)S(1)}, bf16[8,4,384]{2,0,1:T(8,128)(2,1)S(1)}, u32[]{:S(2)}, u32[]{:S(2)}) %collective-permute-start.5) | collective-permute-done | bytes 24608 | tf_op jit(solution)/shard_map/while/body/eval_jaxpr/ppermute | solution.py:30
  (1021 shorter events, 690.2 us)
Async XLA Ops:
  6.5 355.1 %all-gather.6.cloned.1.call-start = ((), (), s32[]{:S(2)}) async-start(), calls=%async_computation.4 | async-start | bytes 6488064 | tf_op jit(solution)/shard_map/all_gather | solution.py:136
  279.4 24.3 %collective-permute-start.10 = (bf16[3,16,1,384]{3,2,1,0:T(2,128)(2,1)}, bf16[3,16,1,384]{3,2,1,0:T(2,128)(2,1)S(1)}, u32[]{:S(2)}, u32[]{:S(2)}) collective-permute-start(bf16[3,16,1,384]{3,2,1,0:T(2,128)(2,1)} %get-tuple-element.963), channel_id=1, source_target_pairs={{0,1},{1,2},{2,3},{3,4},{4,5},{5,6},{6,7},{7,8},{8,9},{9,10},{10,1... | collective-permute-start | bytes 110600 | tf_op jit(solution)/shard_map/ppermute | solution.py:18
  281.3 28.2 %collective-permute-start.11 = (bf16[3,16,1,384]{3,2,1,0:T(2,128)(2,1)}, bf16[3,16,1,384]{3,2,1,0:T(2,128)(2,1)}, u32[]{:S(2)}, u32[]{:S(2)}) collective-permute-start(bf16[3,16,1,384]{3,2,1,0:T(2,128)(2,1)} %get-tuple-element.964), channel_id=1, source_target_pairs={{1,0},{2,1},{3,2},{4,3},{5,4},{6,5},{7,6},{8,7},{9,8},{10,9},{11,1... | collective-permute-start | bytes 110600 | tf_op jit(solution)/shard_map/ppermute | solution.py:20
  288.2 26.5 %collective-permute-start.6 = (bf16[3,16,1,384]{3,2,1,0:T(2,128)(2,1)}, bf16[3,16,1,384]{3,2,1,0:T(2,128)(2,1)S(1)}, u32[]{:S(2)}, u32[]{:S(2)}) collective-permute-start(bf16[3,16,1,384]{3,2,1,0:T(2,128)(2,1)} %get-tuple-element.961), channel_id=1, source_target_pairs={{0,1},{1,2},{2,3},{3,4},{4,5},{5,6},{6,7},{7,8},{8,9},{9,10},{10,1... | collective-permute-start | bytes 110600 | tf_op jit(solution)/shard_map/ppermute | solution.py:18
  290.1 30.6 %collective-permute-start.7 = (bf16[3,16,1,384]{3,2,1,0:T(2,128)(2,1)}, bf16[3,16,1,384]{3,2,1,0:T(2,128)(2,1)S(1)}, u32[]{:S(2)}, u32[]{:S(2)}) collective-permute-start(bf16[3,16,1,384]{3,2,1,0:T(2,128)(2,1)} %get-tuple-element.962), channel_id=1, source_target_pairs={{1,0},{2,1},{3,2},{4,3},{5,4},{6,5},{7,6},{8,7},{9,8},{10,9},{11,1... | collective-permute-start | bytes 110600 | tf_op jit(solution)/shard_map/ppermute | solution.py:20
  295.9 138.5 %all-gather.8.cloned.1.call-start = ((), (), s32[]{:S(2)}) async-start(), calls=%async_computation.5 | async-start | bytes 1622016 | tf_op jit(solution)/shard_map/all_gather | solution.py:160
  301.7 21.4 %collective-permute-start.14 = (bf16[3,16,1,384]{3,2,1,0:T(2,128)(2,1)}, bf16[3,16,1,384]{3,2,1,0:T(2,128)(2,1)S(1)}, u32[]{:S(2)}, u32[]{:S(2)}) collective-permute-start(bf16[3,16,1,384]{3,2,1,0:T(2,128)(2,1)} %get-tuple-element.965), channel_id=1, source_target_pairs={{0,1},{1,2},{2,3},{3,4},{4,5},{5,6},{6,7},{7,8},{8,9},{9,10},{10,1... | collective-permute-start | bytes 110600 | tf_op jit(solution)/shard_map/ppermute | solution.py:18
  303.7 18.5 %collective-permute-start.15 = (bf16[3,16,1,384]{3,2,1,0:T(2,128)(2,1)}, bf16[3,16,1,384]{3,2,1,0:T(2,128)(2,1)S(1)}, u32[]{:S(2)}, u32[]{:S(2)}) collective-permute-start(bf16[3,16,1,384]{3,2,1,0:T(2,128)(2,1)} %get-tuple-element.966), channel_id=1, source_target_pairs={{1,0},{2,1},{3,2},{4,3},{5,4},{6,5},{7,6},{8,7},{9,8},{10,9},{11,1... | collective-permute-start | bytes 110600 | tf_op jit(solution)/shard_map/ppermute | solution.py:20
  372.4 97.6 %all-gather.10.cloned.1.call-start = ((), (), s32[]{:S(2)}) async-start(), calls=%async_computation.7 | async-start | bytes 1622016 | tf_op jit(solution)/shard_map/all_gather | solution.py:160
  393.6 126.2 %all-gather.12.cloned.1.call-start = ((), (), s32[]{:S(2)}) async-start(), calls=%async_computation.9 | async-start | bytes 1622016 | tf_op jit(solution)/shard_map/all_gather | solution.py:160
  414.3 155.4 %all-gather.14.cloned.1.call-start = ((), (), s32[]{:S(2)}) async-start(), calls=%async_computation.11 | async-start | bytes 1622016 | tf_op jit(solution)/shard_map/all_gather | solution.py:160
  434.1 224.8 %reduce-scatter.5.cloned.1.call-start = ((), (), s32[]{:S(2)}) async-start(), calls=%async_computation.6 | async-start | bytes 1622016 | tf_op jit(solution)/shard_map/reduce_scatter | solution.py:180
  460.4 287.8 %reduce-scatter.7.cloned.1.call-start = ((), (), s32[]{:S(2)}) async-start(), calls=%async_computation.8 | async-start | bytes 1622016 | tf_op jit(solution)/shard_map/reduce_scatter | solution.py:180
  495.9 341.6 %reduce-scatter.9.cloned.1.call-start = ((), (), s32[]{:S(2)}) async-start(), calls=%async_computation.10 | async-start | bytes 1622016 | tf_op jit(solution)/shard_map/reduce_scatter | solution.py:180
  545.7 381.2 %reduce-scatter.11.cloned.1.call-start = ((), (), s32[]{:S(2)}) async-start(), calls=%async_computation.12 | async-start | bytes 1622016 | tf_op jit(solution)/shard_map/reduce_scatter | solution.py:180
  659.9 270.0 %collective-permute-start.8 = (bf16[16,1,192]{2,1,0:T(2,128)(2,1)S(1)}, bf16[16,1,192]{2,1,0:T(2,128)(2,1)S(1)}, u32[]{:S(2)}, u32[]{:S(2)}) collective-permute-start(bf16[16,1,192]{2,1,0:T(2,128)(2,1)S(1)} %get-tuple-element.985), channel_id=1, source_target_pairs={{0,1},{1,2},{2,3},{3,4},{4,5},{5,6},{6,7},{7,8},{8,9},{9,10},{10,1... | collective-permute-start | bytes 18440 | tf_op jit(solution)/shard_map/ppermute | solution.py:18
  661.8 273.8 %collective-permute-start.9 = (bf16[16,1,192]{2,1,0:T(2,128)(2,1)S(1)}, bf16[16,1,192]{2,1,0:T(2,128)(2,1)S(1)}, u32[]{:S(2)}, u32[]{:S(2)}) collective-permute-start(bf16[16,1,192]{2,1,0:T(2,128)(2,1)S(1)} %get-tuple-element.986), channel_id=1, source_target_pairs={{1,0},{2,1},{3,2},{4,3},{5,4},{6,5},{7,6},{8,7},{9,8},{10,9},{11,1... | collective-permute-start | bytes 18440 | tf_op jit(solution)/shard_map/ppermute | solution.py:20
  749.2 189.8 %collective-permute-start.12 = (bf16[16,1,192]{2,1,0:T(2,128)(2,1)S(1)}, bf16[16,1,192]{2,1,0:T(2,128)(2,1)S(1)}, u32[]{:S(2)}, u32[]{:S(2)}) collective-permute-start(bf16[16,1,192]{2,1,0:T(2,128)(2,1)S(1)} %get-tuple-element.987), channel_id=1, source_target_pairs={{0,1},{1,2},{2,3},{3,4},{4,5},{5,6},{6,7},{7,8},{8,9},{9,10},{10,1... | collective-permute-start | bytes 18440 | tf_op jit(solution)/shard_map/ppermute | solution.py:18
  751.2 193.7 %collective-permute-start.13 = (bf16[16,1,192]{2,1,0:T(2,128)(2,1)S(1)}, bf16[16,1,192]{2,1,0:T(2,128)(2,1)S(1)}, u32[]{:S(2)}, u32[]{:S(2)}) collective-permute-start(bf16[16,1,192]{2,1,0:T(2,128)(2,1)S(1)} %get-tuple-element.988), channel_id=1, source_target_pairs={{1,0},{2,1},{3,2},{4,3},{5,4},{6,5},{7,6},{8,7},{9,8},{10,9},{11,1... | collective-permute-start | bytes 18440 | tf_op jit(solution)/shard_map/ppermute | solution.py:20
  927.9 24.2 %collective-permute-start.16 = (bf16[16,1,192]{2,1,0:T(2,128)(2,1)S(1)}, bf16[16,1,192]{2,1,0:T(2,128)(2,1)S(1)}, u32[]{:S(2)}, u32[]{:S(2)}) collective-permute-start(bf16[16,1,192]{2,1,0:T(2,128)(2,1)S(1)} %get-tuple-element.989), channel_id=1, source_target_pairs={{0,1},{1,2},{2,3},{3,4},{4,5},{5,6},{6,7},{7,8},{8,9},{9,10},{10,1... | collective-permute-start | bytes 18440 | tf_op jit(solution)/shard_map/ppermute | solution.py:18
  929.9 22.2 %collective-permute-start.17 = (bf16[16,1,192]{2,1,0:T(2,128)(2,1)S(1)}, bf16[16,1,192]{2,1,0:T(2,128)(2,1)S(1)}, u32[]{:S(2)}, u32[]{:S(2)}) collective-permute-start(bf16[16,1,192]{2,1,0:T(2,128)(2,1)S(1)} %get-tuple-element.990), channel_id=1, source_target_pairs={{1,0},{2,1},{3,2},{4,3},{5,4},{6,5},{7,6},{8,7},{9,8},{10,9},{11,1... | collective-permute-start | bytes 18440 | tf_op jit(solution)/shard_map/ppermute | solution.py:20
  937.1 20.6 %collective-permute-start.20 = (bf16[16,1,192]{2,1,0:T(2,128)(2,1)S(1)}, bf16[16,1,192]{2,1,0:T(2,128)(2,1)S(1)}, u32[]{:S(2)}, u32[]{:S(2)}) collective-permute-start(bf16[16,1,192]{2,1,0:T(2,128)(2,1)S(1)} %get-tuple-element.991), channel_id=1, source_target_pairs={{0,1},{1,2},{2,3},{3,4},{4,5},{5,6},{6,7},{7,8},{8,9},{9,10},{10,1... | collective-permute-start | bytes 18440 | tf_op jit(solution)/shard_map/ppermute | solution.py:18
  939.1 18.7 %collective-permute-start.21 = (bf16[16,1,192]{2,1,0:T(2,128)(2,1)S(1)}, bf16[16,1,192]{2,1,0:T(2,128)(2,1)S(1)}, u32[]{:S(2)}, u32[]{:S(2)}) collective-permute-start(bf16[16,1,192]{2,1,0:T(2,128)(2,1)S(1)} %get-tuple-element.992), channel_id=1, source_target_pairs={{1,0},{2,1},{3,2},{4,3},{5,4},{6,5},{7,6},{8,7},{9,8},{10,9},{11,1... | collective-permute-start | bytes 18440 | tf_op jit(solution)/shard_map/ppermute | solution.py:20
  1065.3 35.6 %collective-permute-start.5 = (bf16[8,4,384]{2,0,1:T(8,128)(2,1)S(1)}, bf16[8,4,384]{2,0,1:T(8,128)(2,1)S(1)}, u32[]{:S(2)}, u32[]{:S(2)}) collective-permute-start(bf16[8,4,384]{2,0,1:T(8,128)(2,1)S(1)} %add_convert_fusion.2), channel_id=1, source_target_pairs={{32,0},{64,32},{96,64},{128,96},{160,128},{192,160},{224,192},{33,... | collective-permute-start | bytes 73736 | tf_op jit(solution)/shard_map/while/body/eval_jaxpr/ppermute | solution.py:30
  (85 other events, 648.9 us)
Sparse Core Ops, SparseCore 0:
  296.0 65.5 all-gather.5
  372.5 47.4 all-gather.7
  422.6 47.3 all-gather.9
  472.5 47.3 all-gather.11
  522.3 47.3 all-gather.13
  573.4 85.4 reduce-scatter.4
  662.7 85.4 reduce-scatter.6
  752.0 85.4 reduce-scatter.8
  841.4 85.4 reduce-scatter.10
where the time goes:
time: 1200 us; the launch traced here: 1190 us
  waiting for transfers between devices  546 us (46%)
  starting transfers between devices  237 us (20%)
  local copies, waits for them, and re-layouts  199 us (17%)
  matrix products  119 us (10%)
  other arithmetic  55.6 us (5%)
  loops' own time  21.8 us (2%)
  between operations  15 us (1%)
    reduce_scatter x4, waiting for transfers between devices, on_device(): lax.psum_scatter(patch_back.astype(jnp.bfloat16), 'tile', scatter_dimensi...  278 us
    ppermute x30, waiting for transfers between devices, with_halo(): lax.ppermute(tail, axis, [(i, (i + 1) % count) for i in range(ends)])  93.7 us
    ppermute x22, waiting for transfers between devices, from_behind(): return lax.ppermute(block, axis, route)  92.9 us
    ppermute x30, starting transfers between devices, with_halo(): lax.ppermute(head, axis, [((i + 1) % count, i) for i in range(ends)])  90.8 us
    ppermute x22, starting transfers between devices, from_behind(): return lax.ppermute(block, axis, route)  75.7 us
    ppermute x30, starting transfers between devices, with_halo(): lax.ppermute(tail, axis, [(i, (i + 1) % count) for i in range(ends)])  67.8 us
    all_gather x4, waiting for transfers between devices, on_device(): lax.all_gather(features.reshape(2 * height, 2 * width_dev * up_width), 't...  56.4 us
    unnamed x151, local copies, waits for them, and re-layouts  44.1 us
  transfers between devices with their start and end apart: 91, of which 52 were waited for; matrix products, arithmetic and copies ran while one was open for 21% of the time, Pallas kernels for 0%

commit v1 on v0

--- a/solution.py
+++ b/solution.py
@@ -157,9 +157,9 @@
         )
         preact = preact.reshape(2 * height, 2 * width_dev, up_width)
         features = jax.nn.silu(preact).astype(jnp.bfloat16)
-        gathered = lax.all_gather(
-            features.reshape(2 * height, 2 * width_dev * up_width), "tile", axis=1, tiled=True
-        )
+        block_2 = features.reshape(2 * height, 2 * width_dev * up_width)
+        stack = jnp.stack([block_2] * lax.axis_size("tile"))
+        gathered = jnp.concatenate(lax.all_to_all(stack, "tile", 0, 0), axis=1)
         full_width = gathered.shape[1] // up_width
         patches = (
             gathered.reshape(2 * height // P_SIZE, P_SIZE, full_width // P_SIZE, P_SIZE, up_width)

time: 1200 us -> 1080 us (0.900)
  waiting for transfers between devices: 546 us -> 339 us
  blocking collectives: 0 us -> 28.4 us
  local copies, waits for them, and re-layouts: 199 us -> 225 us
  starting transfers between devices: 237 us -> 256 us
    reduce_scatter x4, waiting for transfers between devices: 278 us -> 96.5 us  [on_device(): lax.psum_scatter(patch_back.astype(jnp.bfloat16), 'tile', scatter_dimensi...]
    all_gather x4 -> x0, waiting for transfers between devices: 56.4 us -> none  [on_device(): lax.all_gather(features.reshape(2 * height, 2 * width_dev * up_width), 't...]
    all_to_all x0 -> x3, waiting for transfers between devices: none -> 40.8 us  [on_device(): gathered = jnp.concatenate(lax.all_to_all(stack, 'tile', 0, 0), axis=1)]
    all_to_all x0 -> x1, blocking collectives: none -> 28.4 us  [on_device(): gathered = jnp.concatenate(lax.all_to_all(stack, 'tile', 0, 0), axis=1)]
    all_to_all x0 -> x3, starting transfers between devices: none -> 20.7 us  [on_device(): gathered = jnp.concatenate(lax.all_to_all(stack, 'tile', 0, 0), axis=1)]
    another operation x18 -> x30, local copies, waits for them, and re-layouts: 0.2 us -> 20.6 us  [the longest x4 15.7 us: on_device(): gathered.reshape(2 * height // P_SIZE, P_SIZE, full_width // P_SIZE, P_SI...]
    unnamed x151 -> x147, local copies, waits for them, and re-layouts: 44.1 us -> 42.3 us
  transfers between devices with their start and end apart: 91 -> 90, of which waited for: 52 -> 50; matrix products, arithmetic and copies ran while one was open for 21% -> 23% of each run, Pallas kernels for 0% -> 0%
where the time goes in v1:
time: 1080 us; the launch traced here: 1070 us
  waiting for transfers between devices  339 us (31%)
  starting transfers between devices  256 us (24%)
  local copies, waits for them, and re-layouts  225 us (21%)
  matrix products  119 us (11%)
  other arithmetic  58 us (5%)
  blocking collectives  28.4 us (3%)
  loops' own time  24.6 us (2%)
  between operations  15 us (1%)
    reduce_scatter x4, waiting for transfers between devices, on_device(): lax.psum_scatter(patch_back.astype(jnp.bfloat16), 'tile', scatter_dimensi...  96.5 us
    ppermute x30, waiting for transfers between devices, with_halo(): lax.ppermute(tail, axis, [(i, (i + 1) % count) for i in range(ends)])  94.1 us
    ppermute x22, waiting for transfers between devices, from_behind(): return lax.ppermute(block, axis, route)  93.3 us
    ppermute x30, starting transfers between devices, with_halo(): lax.ppermute(head, axis, [((i + 1) % count, i) for i in range(ends)])  90.3 us
    ppermute x22, starting transfers between devices, from_behind(): return lax.ppermute(block, axis, route)  75.7 us
    ppermute x30, starting transfers between devices, with_halo(): lax.ppermute(tail, axis, [(i, (i + 1) % count) for i in range(ends)])  68.5 us
    convert_element_type x12, local copies, waits for them, and re-layouts, on_device(): patch_back.astype(jnp.bfloat16)  44.5 us
    unnamed x147, local copies, waits for them, and re-layouts  42.3 us
  transfers between devices with their start and end apart: 90, of which 50 were waited for; matrix products, arithmetic and copies ran while one was open for 23% of the time, Pallas kernels for 0%

profile of v1, /device:TPU:2, one launch (start us, length us, event | category | flops | bytes accessed | tf_op | source)
XLA Modules:
  0.0 1065.6 jit_solution(6767570335978162468)
XLA Ops:
  7.3 276.3 %while.49 = (s32[]{:T(128)}, bf16[8,6,384]{2,0,1:T(8,128)(2,1)S(1)}, bf16[8,6,384]{2,0,1:T(8,128)(2,1)S(1)}, bf16[8,4,384]{2,0,1:T(8,128)(2,1)S(1)}, bf16[4,8,4,...) while((s32[]{:T(128)}, ...), condition=%wide.region_5.6_spmd.clone, body=%wide.region_0.5_spmd.clone.sunk | while | flops 255259072 | bytes 13963990 | solution.py:133
  129.7 9.3 collective-permute-start.2
  271.6 10.5 collective-permute-start.2
  352.6 14.4 %all-gather.2.cloned.1.call-done = bf16[27,384,192]{2,0,1:T(8,128)(2,1)} async-done(((bf16[27,12,192]{2,0,1:T(8,128)(2,1)}), bf16[27,384,192]{2,0,1:T(8,128)(2,1)}) %all-gather.2.cloned.1.call-update) | async-done | bytes 3981328 | tf_op jit(solution)/shard_map/all_gather | solution.py:136
  367.0 10.1 multiply_convert_fusion.7
  392.2 12.6 %all-to-all-done = bf16[32,16,1536]{2,1,0:T(8,128)(2,1)} async-done(((bf16[32,16,1536]{2,1,0:T(8,128)(2,1)}), bf16[32,16,1536]{2,1,0:T(8,128)(2,1)}, u32[]{:S(2)}, u32[]{:S(2)}) %all-to-all-start) | async-done | bytes 1572896 | tf_op jit(solution)/shard_map/all_to_all | solution.py:162
  420.2 7.7 convolution_convert_fusion.3
  440.5 9.4 multiply_convert_fusion.5
  451.4 7.4 all-to-all-start.1
  464.6 14.5 %all-to-all-done.1 = bf16[32,16,1536]{2,1,0:T(8,128)(2,1)} async-done(((bf16[32,16,1536]{2,1,0:T(8,128)(2,1)}), bf16[32,16,1536]{2,1,0:T(8,128)(2,1)}, u32[]{:S(2)}, u32[]{:S(2)}) %all-to-all-start.1) | async-done | bytes 1572896 | tf_op jit(solution)/shard_map/all_to_all | solution.py:162
  495.0 7.8 convolution_convert_fusion.2
  515.4 9.4 multiply_convert_fusion.3
  526.3 7.2 all-to-all-start.2
  540.0 13.7 %all-to-all-done.2 = bf16[32,16,1536]{2,1,0:T(8,128)(2,1)} async-done(((bf16[32,16,1536]{2,1,0:T(8,128)(2,1)}), bf16[32,16,1536]{2,1,0:T(8,128)(2,1)}, u32[]{:S(2)}, u32[]{:S(2)}) %all-to-all-start.2) | async-done | bytes 1572896 | tf_op jit(solution)/shard_map/all_to_all | solution.py:162
  566.1 7.3 convolution_convert_fusion.1
  583.4 9.5 multiply_convert_fusion.1
  593.2 28.4 %all_to_all.20 = bf16[32,16,1536]{2,1,0:T(8,128)(2,1)S(1)} all-to-all(bf16[32,16,1536]{2,1,0:T(8,128)(2,1)S(1)} %stack.270), channel_id=1, replica_groups=mesh['segment'=8,'tile'=32] {'tile'}, dimensions={0} | all-to-all | bytes 3145728 | tf_op jit(solution)/shard_map/all_to_all | solution.py:162
  632.3 7.3 convolution_convert_fusion
  649.4 11.5 %copy.651 = bf16[27,384,384]{2,1,0:T(8,128)(2,1)} copy(bf16[27,384,384]{1,2,0:T(8,128)(2,1)} %bitcast.1100) | data formatting | bytes 15925248 | tf_op jit(solution)/shard_map/transpose | solution.py:86
  661.0 8.7 copy.546
  701.8 8.3 reduce-scatter.9.cloned.1.call-done
  711.1 88.2 %reduce-scatter.11.cloned.1.call-done = bf16[16,1536]{1,0:T(8,128)(2,1)} async-done(((bf16[16,49152]{1,0:T(8,128)(2,1)}), bf16[16,1536]{1,0:T(8,128)(2,1)}) %reduce-scatter.11.cloned.1.call-update) | async-done | bytes 49168 | tf_op jit(solution)/shard_map/reduce_scatter | solution.py:180
  836.9 221.2 %while.50 = (s32[]{:T(128)}, bf16[8,6,384]{2,0,1:T(8,128)(2,1)S(1)}, bf16[8,6,384]{2,0,1:T(8,128)(2,1)S(1)}, f32[8,4,384]{2,0,1:T(8,128)S(1)}, f32[4,8,4,384]{3,...) while((s32[]{:T(128)}, ...), condition=%wide.region_20.21_spmd.clone, body=%wide.region_14.20_spmd.clone.sunk | while | flops 255418992 | bytes 14603769 | solution.py:243
  939.9 33.6 %collective-permute-done.5 = bf16[8,4,384]{2,0,1:T(8,128)(2,1)S(1)} collective-permute-done((bf16[8,4,384]{2,0,1:T(8,128)(2,1)S(1)}, bf16[8,4,384]{2,0,1:T(8,128)(2,1)S(1)}, u32[]{:S(2)}, u32[]{:S(2)}) %collective-permute-start.5) | collective-permute-done | bytes 24608 | tf_op jit(solution)/shard_map/while/body/eval_jaxpr/ppermute | solution.py:30
  (1020 shorter events, 731.4 us)
Async XLA Ops:
  6.5 360.5 %all-gather.2.cloned.1.call-start = ((), (), s32[]{:S(2)}) async-start(), calls=%async_computation.8 | async-start | bytes 6488064 | tf_op jit(solution)/shard_map/all_gather | solution.py:136
  285.3 24.2 %collective-permute-start.10 = (bf16[3,16,1,384]{3,2,1,0:T(2,128)(2,1)}, bf16[3,16,1,384]{3,2,1,0:T(2,128)(2,1)S(1)}, u32[]{:S(2)}, u32[]{:S(2)}) collective-permute-start(bf16[3,16,1,384]{3,2,1,0:T(2,128)(2,1)} %get-tuple-element.963), channel_id=1, source_target_pairs={{0,1},{1,2},{2,3},{3,4},{4,5},{5,6},{6,7},{7,8},{8,9},{9,10},{10,1... | collective-permute-start | bytes 110600 | tf_op jit(solution)/shard_map/ppermute | solution.py:18
  287.2 28.1 %collective-permute-start.11 = (bf16[3,16,1,384]{3,2,1,0:T(2,128)(2,1)}, bf16[3,16,1,384]{3,2,1,0:T(2,128)(2,1)}, u32[]{:S(2)}, u32[]{:S(2)}) collective-permute-start(bf16[3,16,1,384]{3,2,1,0:T(2,128)(2,1)} %get-tuple-element.964), channel_id=1, source_target_pairs={{1,0},{2,1},{3,2},{4,3},{5,4},{6,5},{7,6},{8,7},{9,8},{10,9},{11,1... | collective-permute-start | bytes 110600 | tf_op jit(solution)/shard_map/ppermute | solution.py:20
  294.1 25.9 %collective-permute-start.6 = (bf16[3,16,1,384]{3,2,1,0:T(2,128)(2,1)}, bf16[3,16,1,384]{3,2,1,0:T(2,128)(2,1)S(1)}, u32[]{:S(2)}, u32[]{:S(2)}) collective-permute-start(bf16[3,16,1,384]{3,2,1,0:T(2,128)(2,1)} %get-tuple-element.961), channel_id=1, source_target_pairs={{0,1},{1,2},{2,3},{3,4},{4,5},{5,6},{6,7},{7,8},{8,9},{9,10},{10,1... | collective-permute-start | bytes 110600 | tf_op jit(solution)/shard_map/ppermute | solution.py:18
  296.0 29.9 %collective-permute-start.7 = (bf16[3,16,1,384]{3,2,1,0:T(2,128)(2,1)}, bf16[3,16,1,384]{3,2,1,0:T(2,128)(2,1)}, u32[]{:S(2)}, u32[]{:S(2)}) collective-permute-start(bf16[3,16,1,384]{3,2,1,0:T(2,128)(2,1)} %get-tuple-element.962), channel_id=1, source_target_pairs={{1,0},{2,1},{3,2},{4,3},{5,4},{6,5},{7,6},{8,7},{9,8},{10,9},{11,1... | collective-permute-start | bytes 110600 | tf_op jit(solution)/shard_map/ppermute | solution.py:20
  307.5 21.5 %collective-permute-start.14 = (bf16[3,16,1,384]{3,2,1,0:T(2,128)(2,1)}, bf16[3,16,1,384]{3,2,1,0:T(2,128)(2,1)S(1)}, u32[]{:S(2)}, u32[]{:S(2)}) collective-permute-start(bf16[3,16,1,384]{3,2,1,0:T(2,128)(2,1)} %get-tuple-element.965), channel_id=1, source_target_pairs={{0,1},{1,2},{2,3},{3,4},{4,5},{5,6},{6,7},{7,8},{8,9},{9,10},{10,1... | collective-permute-start | bytes 110600 | tf_op jit(solution)/shard_map/ppermute | solution.py:18
  309.5 19.7 %collective-permute-start.15 = (bf16[3,16,1,384]{3,2,1,0:T(2,128)(2,1)}, bf16[3,16,1,384]{3,2,1,0:T(2,128)(2,1)S(1)}, u32[]{:S(2)}, u32[]{:S(2)}) collective-permute-start(bf16[3,16,1,384]{3,2,1,0:T(2,128)(2,1)} %get-tuple-element.966), channel_id=1, source_target_pairs={{1,0},{2,1},{3,2},{4,3},{5,4},{6,5},{7,6},{8,7},{9,8},{10,9},{11,1... | collective-permute-start | bytes 110600 | tf_op jit(solution)/shard_map/ppermute | solution.py:20
  318.0 24.5 %collective-permute-start.18 = (bf16[3,16,1,384]{3,2,1,0:T(2,128)(2,1)}, bf16[3,16,1,384]{3,2,1,0:T(2,128)(2,1)S(1)}, u32[]{:S(2)}, u32[]{:S(2)}) collective-permute-start(bf16[3,16,1,384]{3,2,1,0:T(2,128)(2,1)} %get-tuple-element.967), channel_id=1, source_target_pairs={{0,1},{1,2},{2,3},{3,4},{4,5},{5,6},{6,7},{7,8},{8,9},{9,10},{10,1... | collective-permute-start | bytes 110600 | tf_op jit(solution)/shard_map/ppermute | solution.py:18
  319.9 21.8 %collective-permute-start.19 = (bf16[3,16,1,384]{3,2,1,0:T(2,128)(2,1)}, bf16[3,16,1,384]{3,2,1,0:T(2,128)(2,1)S(1)}, u32[]{:S(2)}, u32[]{:S(2)}) collective-permute-start(bf16[3,16,1,384]{3,2,1,0:T(2,128)(2,1)} %get-tuple-element.968), channel_id=1, source_target_pairs={{1,0},{2,1},{3,2},{4,3},{5,4},{6,5},{7,6},{8,7},{9,8},{10,9},{11,1... | collective-permute-start | bytes 110600 | tf_op jit(solution)/shard_map/ppermute | solution.py:20
  378.5 26.2 %all-to-all-start = ((bf16[32,16,1536]{2,1,0:T(8,128)(2,1)}), bf16[32,16,1536]{2,1,0:T(8,128)(2,1)}, u32[]{:S(2)}, u32[]{:S(2)}) async-start(bf16[32,16,1536]{2,1,0:T(8,128)(2,1)} %stack.234), calls=%async_computation | async-start | bytes 3145728 | tf_op jit(solution)/shard_map/all_to_all | solution.py:162
  384.6 299.8 %reduce-scatter.5.cloned.1.call-start = ((), (), s32[]{:S(2)}) async-start(), calls=%async_computation.9 | async-start | bytes 1622016 | tf_op jit(solution)/shard_map/reduce_scatter | solution.py:180
  451.4 27.7 %all-to-all-start.1 = ((bf16[32,16,1536]{2,1,0:T(8,128)(2,1)}), bf16[32,16,1536]{2,1,0:T(8,128)(2,1)}, u32[]{:S(2)}, u32[]{:S(2)}) async-start(bf16[32,16,1536]{2,1,0:T(8,128)(2,1)} %stack.246), calls=%async_computation.2 | async-start | bytes 3145728 | tf_op jit(solution)/shard_map/all_to_all | solution.py:162
  458.8 234.3 %reduce-scatter.7.cloned.1.call-start = ((), (), s32[]{:S(2)}) async-start(), calls=%async_computation.10 | async-start | bytes 1622016 | tf_op jit(solution)/shard_map/reduce_scatter | solution.py:180
  526.3 27.5 %all-to-all-start.2 = ((bf16[32,16,1536]{2,1,0:T(8,128)(2,1)}), bf16[32,16,1536]{2,1,0:T(8,128)(2,1)}, u32[]{:S(2)}, u32[]{:S(2)}) async-start(bf16[32,16,1536]{2,1,0:T(8,128)(2,1)} %stack.258), calls=%async_computation.4 | async-start | bytes 3145728 | tf_op jit(solution)/shard_map/all_to_all | solution.py:162
  533.5 176.6 %reduce-scatter.9.cloned.1.call-start = ((), (), s32[]{:S(2)}) async-start(), calls=%async_computation.11 | async-start | bytes 1622016 | tf_op jit(solution)/shard_map/reduce_scatter | solution.py:180
  583.1 216.1 %reduce-scatter.11.cloned.1.call-start = ((), (), s32[]{:S(2)}) async-start(), calls=%async_computation.12 | async-start | bytes 1622016 | tf_op jit(solution)/shard_map/reduce_scatter | solution.py:180
  685.4 116.8 %collective-permute-start.8 = (bf16[16,1,192]{2,1,0:T(2,128)(2,1)S(1)}, bf16[16,1,192]{2,1,0:T(2,128)(2,1)S(1)}, u32[]{:S(2)}, u32[]{:S(2)}) collective-permute-start(bf16[16,1,192]{2,1,0:T(2,128)(2,1)S(1)} %get-tuple-element.985), channel_id=1, source_target_pairs={{0,1},{1,2},{2,3},{3,4},{4,5},{5,6},{6,7},{7,8},{8,9},{9,10},{10,1... | collective-permute-start | bytes 18440 | tf_op jit(solution)/shard_map/ppermute | solution.py:18
  688.0 119.9 %collective-permute-start.9 = (bf16[16,1,192]{2,1,0:T(2,128)(2,1)S(1)}, bf16[16,1,192]{2,1,0:T(2,128)(2,1)S(1)}, u32[]{:S(2)}, u32[]{:S(2)}) collective-permute-start(bf16[16,1,192]{2,1,0:T(2,128)(2,1)S(1)} %get-tuple-element.986), channel_id=1, source_target_pairs={{1,0},{2,1},{3,2},{4,3},{5,4},{6,5},{7,6},{8,7},{9,8},{10,9},{11,1... | collective-permute-start | bytes 18440 | tf_op jit(solution)/shard_map/ppermute | solution.py:20
  694.1 117.3 %collective-permute-start.12 = (bf16[16,1,192]{2,1,0:T(2,128)(2,1)S(1)}, bf16[16,1,192]{2,1,0:T(2,128)(2,1)S(1)}, u32[]{:S(2)}, u32[]{:S(2)}) collective-permute-start(bf16[16,1,192]{2,1,0:T(2,128)(2,1)S(1)} %get-tuple-element.987), channel_id=1, source_target_pairs={{0,1},{1,2},{2,3},{3,4},{4,5},{5,6},{6,7},{7,8},{8,9},{9,10},{10,1... | collective-permute-start | bytes 18440 | tf_op jit(solution)/shard_map/ppermute | solution.py:18
  696.0 121.4 %collective-permute-start.13 = (bf16[16,1,192]{2,1,0:T(2,128)(2,1)S(1)}, bf16[16,1,192]{2,1,0:T(2,128)(2,1)S(1)}, u32[]{:S(2)}, u32[]{:S(2)}) collective-permute-start(bf16[16,1,192]{2,1,0:T(2,128)(2,1)S(1)} %get-tuple-element.988), channel_id=1, source_target_pairs={{1,0},{2,1},{3,2},{4,3},{5,4},{6,5},{7,6},{8,7},{9,8},{10,9},{11,1... | collective-permute-start | bytes 18440 | tf_op jit(solution)/shard_map/ppermute | solution.py:20
  800.3 24.4 %collective-permute-start.16 = (bf16[16,1,192]{2,1,0:T(2,128)(2,1)S(1)}, bf16[16,1,192]{2,1,0:T(2,128)(2,1)S(1)}, u32[]{:S(2)}, u32[]{:S(2)}) collective-permute-start(bf16[16,1,192]{2,1,0:T(2,128)(2,1)S(1)} %get-tuple-element.989), channel_id=1, source_target_pairs={{0,1},{1,2},{2,3},{3,4},{4,5},{5,6},{6,7},{7,8},{8,9},{9,10},{10,1... | collective-permute-start | bytes 18440 | tf_op jit(solution)/shard_map/ppermute | solution.py:18
  802.2 22.4 %collective-permute-start.17 = (bf16[16,1,192]{2,1,0:T(2,128)(2,1)S(1)}, bf16[16,1,192]{2,1,0:T(2,128)(2,1)S(1)}, u32[]{:S(2)}, u32[]{:S(2)}) collective-permute-start(bf16[16,1,192]{2,1,0:T(2,128)(2,1)S(1)} %get-tuple-element.990), channel_id=1, source_target_pairs={{1,0},{2,1},{3,2},{4,3},{5,4},{6,5},{7,6},{8,7},{9,8},{10,9},{11,1... | collective-permute-start | bytes 18440 | tf_op jit(solution)/shard_map/ppermute | solution.py:20
  809.5 20.8 %collective-permute-start.20 = (bf16[16,1,192]{2,1,0:T(2,128)(2,1)S(1)}, bf16[16,1,192]{2,1,0:T(2,128)(2,1)S(1)}, u32[]{:S(2)}, u32[]{:S(2)}) collective-permute-start(bf16[16,1,192]{2,1,0:T(2,128)(2,1)S(1)} %get-tuple-element.991), channel_id=1, source_target_pairs={{0,1},{1,2},{2,3},{3,4},{4,5},{5,6},{6,7},{7,8},{8,9},{9,10},{10,1... | collective-permute-start | bytes 18440 | tf_op jit(solution)/shard_map/ppermute | solution.py:18
  937.9 35.6 %collective-permute-start.5 = (bf16[8,4,384]{2,0,1:T(8,128)(2,1)S(1)}, bf16[8,4,384]{2,0,1:T(8,128)(2,1)S(1)}, u32[]{:S(2)}, u32[]{:S(2)}) collective-permute-start(bf16[8,4,384]{2,0,1:T(8,128)(2,1)S(1)} %add_convert_fusion.2), channel_id=1, source_target_pairs={{32,0},{64,32},{96,64},{128,96},{160,128},{192,160},{224,192},{33,... | collective-permute-start | bytes 73736 | tf_op jit(solution)/shard_map/while/body/eval_jaxpr/ppermute | solution.py:30
  (82 other events, 487.6 us)
Sparse Core Ops, SparseCore 0:
  301.9 65.0 all-gather.1
  440.6 85.9 reduce-scatter.4
  530.4 89.1 reduce-scatter.6
  623.3 86.7 reduce-scatter.8
  713.8 85.4 reduce-scatter.10
